TPU v7x, 32 devices: a whole 2x2x4 slice. The times are simulated.
32 devices in a mesh: fx: 2 (over y), fy: 4 (over x, core), st: 4 (over z).
Axes of the slice: x: 2, y: 2, z: 4, core: 2. Of those that a mesh axis runs over, the one named last changes fastest.
Arguments:
- tangent_rhs: bfloat16 [4, 6, 64, 2, 4, 128], P('st', None, None, 'fx', 'fy'), may hold values from -6 to 6
- adjoint_rhs: bfloat16 [4, 6, 64, 2, 4, 128], P('st', None, None, 'fx', 'fy'), may hold values from -6 to 6
- jacobians: bfloat16 [3, 6, 6, 2, 4, 128], P(None, None, None, 'fx', 'fy'), may hold values from -0.75 to 0.75
- deriv: bfloat16 [3, 64, 64], replicated, may hold values from -0.75 to 0.75
- penalty: float32 [6], replicated, may hold values from 0.1 to 0.4
- second_order: float32 [6, 2, 4, 128], P(None, 'fx', 'fy'), may hold values from -4 to 4
- coupling: bfloat16 [6, 384], replicated, may hold values from -2.5 to 2.5
- shell_inverse: bfloat16 [16, 384, 384], P('st')
- shell_load: float32 [4, 16, 384], P(None, 'st'), may hold values from -6 to 6
- shell_adjoint_rhs: float32 [4, 16, 384], P(None, 'st'), may hold values from -6 to 6
- iface_elem: int32 [8, 128], P(('fx', 'fy')), may hold values from 0 to 127
- iface_node: int32 [8, 128], P(('fx', 'fy')), may hold values from 0 to 1023
- iface_weight: float32 [8, 128], P(('fx', 'fy')), may hold values from 0.5 to 2
- iface_count: int32 [8], P(('fx', 'fy')), may hold values from 0 to 128, as said below
Outputs:
- tangent_flow: bfloat16 [4, 6, 64, 2, 4, 128], P('st', None, None, 'fx', 'fy')
- adjoint_flow: bfloat16 [4, 6, 64, 2, 4, 128], P('st', None, None, 'fx', 'fy')
- shell_tangent: float32 [4, 16, 384], P(None, 'st')
- shell_adjoint: float32 [4, 16, 384], P(None, 'st')
Inputs may be any that keep to these rules, and one draw needn't show every extreme that they name: `iface_count`: at most 128 live slots in one flow block; some block has exactly 128.
All inputs are finite; a program needn't handle non-finite values.
Results may differ from a plain program's by a relative error of at most 0.0069.
Values may be sent and summed in bfloat16 or wider, within the bound.
No kernel may reach another device: no remote copies, remote signals or barrier semaphores. Data moves between devices by JAX's collectives and lax.ppermute only.
A program may use at most 64 MiB of HBM per device.

v0:
```python
import jax
import jax.numpy as jnp
from jax import lax
from jax.sharding import PartitionSpec as P

SDOF = 6
PN = 64
FSWEEP = 3
ROUNDS = 2
SIGMA = 0.5


def with_halo(value, sides, width):
    for axis, dim in sides:
        peers, length = (lax.axis_size(axis), value.shape[dim])
        up = [(i, (i + 1) % peers) for i in range(peers - 1)]
        down = [(j, i) for i, j in up]
        last = lax.slice_in_dim(value, length - width, length, axis=dim)
        initial = lax.slice_in_dim(value, 0, width, axis=dim)
        before = lax.ppermute(last, axis, up)
        after = lax.ppermute(initial, axis, down)
        value = jnp.concatenate([before, value, after], axis=dim)
    return value


def face_pair(lower_face, upper_face, below, above, axis):
    length = lower_face.shape[axis]
    beyond_upper = jnp.concatenate(
        [lax.slice_in_dim(lower_face, 1, length, axis=axis), above], axis=axis
    )
    beyond_lower = jnp.concatenate(
        [below, lax.slice_in_dim(upper_face, 0, length - 1, axis=axis)], axis=axis
    )
    return (lower_face - beyond_lower, upper_face - beyond_upper)


def place_faces(jump_low, jump_high, axis):
    middle_shape = list(jump_low.shape)
    middle_shape.insert(axis, 2)
    middle = jnp.zeros(middle_shape, jump_low.dtype)
    return jnp.concatenate(
        [jnp.expand_dims(jump_low, axis), middle, jnp.expand_dims(jump_high, axis)], axis=axis
    )


def as_cube(values):
    members, variables, points, size_x, size_y, size_z = values.shape
    return values.reshape(members, variables, 4, 4, 4, size_x, size_y, size_z)


def face_edges(values):
    cube = as_cube(values)
    received = []
    for node_axis in (2, 3):
        elem_axis = node_axis + 2
        lower_face = jnp.take(cube, 0, axis=node_axis)
        upper_face = jnp.take(cube, 3, axis=node_axis)
        edges = jnp.concatenate([lower_face, upper_face], axis=elem_axis)
        if node_axis == 2:
            extended = with_halo(edges, (("fx", 4),), 1)
        else:
            extended = with_halo(edges, (("fy", 5),), 1)
        below = lax.slice_in_dim(extended, 0, 1, axis=elem_axis)
        above = lax.slice_in_dim(extended, 3, 4, axis=elem_axis)
        received.append((below, above))
    return received


def flow_jumps(values, received):
    cube = as_cube(values)
    result = jnp.zeros(cube.shape, jnp.float32)
    for node_axis in (2, 3, 4):
        elem_axis = node_axis + 2
        lower_face = jnp.take(cube, 0, axis=node_axis).astype(jnp.float32)
        upper_face = jnp.take(cube, 3, axis=node_axis).astype(jnp.float32)
        if received is None or node_axis == 4:
            below = jnp.zeros_like(lax.slice_in_dim(lower_face, 0, 1, axis=elem_axis))
            above = below
        else:
            below = received[node_axis - 2][0].astype(jnp.float32)
            above = received[node_axis - 2][1].astype(jnp.float32)
        jump_low, jump_high = face_pair(lower_face, upper_face, below, above, elem_axis)
        result = result + place_faces(jump_low, jump_high, node_axis)
    return result.reshape(values.shape)


def volume(values, deriv_mats, jac_mats):
    grads = jnp.einsum("kpq,vqxyz->kvpxyz", deriv_mats, values, preferred_element_type=jnp.float32)
    result = jnp.sum(jac_mats[0][:, :, None] * grads[0][None], axis=1)
    for axis_index in (1, 2):
        result = result + jnp.sum(
            jac_mats[axis_index][:, :, None] * grads[axis_index][None], axis=1
        )
    return result


def operator(states, operator_kinds, penalty):
    values = lax.optimization_barrier(states.astype(jnp.bfloat16))
    received = face_edges(values)
    jumps = flow_jumps(values, received)
    volumes = jnp.stack(
        [
            volume(values[member], operator_kinds[member][0], operator_kinds[member][1])
            for member in range(len(operator_kinds))
        ]
    )
    return states + volumes + penalty[None, :, None, None, None, None] * jumps


def body(
    tangent_rhs,
    adjoint_rhs,
    jacobians,
    deriv,
    penalty,
    second_order,
    coupling,
    shell_inverse,
    shell_load,
    shell_adjoint_rhs,
    iface_elem,
    iface_node,
    iface_weight,
    iface_count,
):
    state_shape = tangent_rhs.shape
    variables = state_shape[1]
    points = state_shape[2]
    elements = state_shape[3] * state_shape[4] * state_shape[5]
    slots = iface_elem.shape[1]
    live = (jnp.arange(slots, dtype=jnp.int32) < iface_count[0]).astype(jnp.float32)
    weights = iface_weight[0] * live
    elem_index = iface_elem[0]
    node_index = iface_node[0]
    dof_rows = jnp.arange(SDOF, dtype=jnp.int32)[:, None]
    columns = (node_index // PN)[None, :] * (SDOF * PN) + dof_rows * PN + (node_index % PN)[None, :]
    forward_jac = jacobians.astype(jnp.float32)
    forward_kind = (deriv, forward_jac)
    backward_kind = (jnp.swapaxes(deriv, 1, 2), jnp.swapaxes(forward_jac, 1, 2))
    coupling_cols = coupling.T

    def shell_solve(rhs):
        return jnp.einsum(
            "pab,dpb->dpa",
            shell_inverse,
            rhs.astype(jnp.bfloat16),
            preferred_element_type=jnp.float32,
        )

    shell_tangent = shell_solve(shell_load)
    shell_adjoint = jnp.zeros(shell_load.shape, jnp.float32)
    tangent = jnp.zeros(state_shape, jnp.float32)
    adjoint = jnp.zeros(state_shape, jnp.float32)
    for round_index in range(ROUNDS):
        received = lax.all_to_all(
            shell_tangent.astype(jnp.bfloat16), "st", split_axis=0, concat_axis=1, tiled=True
        )
        picked = received.reshape(-1)[columns]
        pushed_cols = (
            jnp.dot(coupling_cols, picked, preferred_element_type=jnp.float32) * weights[None, :]
        )
        pushed = (
            jnp.zeros((variables * points, elements), jnp.float32)
            .at[:, elem_index]
            .add(pushed_cols)
        )
        force = tangent_rhs.astype(jnp.float32) - pushed.reshape(state_shape)
        adjoint_source = adjoint_rhs.astype(jnp.float32) + second_order[None, :, None] * tangent
        paired = jnp.concatenate([tangent, adjoint])
        sources = jnp.concatenate([force, adjoint_source])
        for sweep in range(FSWEEP):
            paired = paired + SIGMA * (
                sources - operator(paired, (forward_kind, backward_kind), penalty)
            )
        tangent = paired[:1]
        adjoint = paired[1:]
        adjoint_values = adjoint.astype(jnp.bfloat16).reshape(variables * points, elements)
        gathered = adjoint_values[:, elem_index]
        loads = jnp.dot(coupling, gathered, preferred_element_type=jnp.float32) * weights[None, :]
        panels = received.shape[1]
        partial_loads = jnp.zeros((panels * SDOF * PN,), jnp.float32).at[columns].add(loads)
        partial_loads = partial_loads.reshape(1, panels, SDOF * PN)
        summed = lax.psum(partial_loads, ("fx", "fy"))
        owned = lax.all_to_all(summed, "st", split_axis=1, concat_axis=0, tiled=True)
        shell_adjoint = shell_solve(shell_adjoint_rhs - owned)
        shell_tangent = shell_solve(shell_load + shell_adjoint)
    return (
        tangent.astype(jnp.bfloat16),
        adjoint.astype(jnp.bfloat16),
        shell_tangent,
        shell_adjoint,
    )


def solution(mesh):
    in_specs = (
        P("st", None, None, "fx", "fy", None),
        P("st", None, None, "fx", "fy", None),
        P(None, None, None, "fx", "fy", None),
        P(),
        P(),
        P(None, "fx", "fy", None),
        P(),
        P("st", None, None),
        P(None, "st", None),
        P(None, "st", None),
        P(("fx", "fy"), None),
        P(("fx", "fy"), None),
        P(("fx", "fy"), None),
        P(("fx", "fy")),
    )
    out_specs = (
        P("st", None, None, "fx", "fy", None),
        P("st", None, None, "fx", "fy", None),
        P(None, "st", None),
        P(None, "st", None),
    )
    return jax.shard_map(body, mesh=mesh, in_specs=in_specs, out_specs=out_specs, check_vma=False)
```

profile of v0, /device:TPU:0, one launch (start us, length us, event | category | flops | bytes accessed | tf_op | source)
XLA Modules:
  0.0 207.5 jit_solution(6584082621477791752)
XLA Ops:
  0.7 5.0 %collective-permute-start = (bf16[2,6,4,4,1,1,128]{6,3,2,1,0,5,4:T(4,128)(2,1)S(1)}, bf16[2,6,4,4,1,1,128]{6,3,2,1,0,5,4:T(4,128)(2,1)S(1)}, u32[]{:S(2)}, u32[]{:S(2)}) collective-permute-start(bf16[2,6,4,4,1,1,128]{6,3,2,1,0,5,4:T(4,128)(2,1)S(1)} %get-tuple-element.197), channel_id=1, source_target_pairs={{0,16},{1,17},{2,18},{3,19},{4,20},{5,21},{6,22},{7,23},{8,24},{9,... | collective-permute-start | bytes 147464 | tf_op jit(solution)/shard_map/ppermute | solution.py:20
  5.8 1.3 collective-permute-start.1
  7.1 1.5 collective-permute-start.2
  11.7 4.9 %all-to-all-start = ((bf16[4,4,384]{2,1,0:T(4,128)(2,1)}), bf16[4,4,384]{2,1,0:T(4,128)(2,1)S(1)}, u32[]{:S(2)}, u32[]{:S(2)}) async-start(bf16[4,4,384]{2,1,0:T(4,128)(2,1)} %copy.260), calls=%async_computation | async-start | bytes 24576 | tf_op jit(solution)/shard_map/all_to_all | solution.py:155
  22.2 5.0 %gather_fusion = bf16[768]{0:T(1024)(128)(2,1)S(1)} fusion(bf16[6144]{0:T(1024)(128)(2,1)S(1)} %reshape.2599, s32[1024]{0:T(1024)S(1)} %pad_clamp_fusion.1), kind=kCustom, calls=%fused_computation | custom fusion | bytes 6144 | tf_op jit(solution)/shard_map/gather | solution.py:158
  27.5 1.4 scatter_custom_fusion
  31.5 4.4 %collective-permute-start.4 = (bf16[2,6,4,4,1,1,128]{6,3,2,1,0,5,4:T(4,128)(2,1)S(1)}, bf16[2,6,4,4,1,1,128]{6,3,2,1,0,5,4:T(4,128)(2,1)S(1)}, u32[]{:S(2)}, u32[]{:S(2)}) collective-permute-start(bf16[2,6,4,4,1,1,128]{6,3,2,1,0,5,4:T(4,128)(2,1)S(1)} %get-tuple-element.187), channel_id=1, source_target_pairs={{0,16},{1,17},{2,18},{3,19},{4,20},{5,21},{6,22},{7,23},{8,24},{9,... | collective-permute-start | bytes 147464 | tf_op jit(solution)/shard_map/ppermute | solution.py:20
  37.2 3.0 %collective-permute-start.6 = (bf16[2,6,4,4,1,1,128]{6,3,2,1,0,5,4:T(4,128)(2,1)S(1)}, bf16[2,6,4,4,1,1,128]{6,3,2,1,0,5,4:T(4,128)(2,1)S(1)}, u32[]{:S(2)}, u32[]{:S(2)}) collective-permute-start(bf16[2,6,4,4,1,1,128]{6,3,2,1,0,5,4:T(4,128)(2,1)S(1)} %get-tuple-element.185), channel_id=1, source_target_pairs={{0,4},{4,8},{8,12},{1,5},{5,9},{9,13},{2,6},{6,10},{10,14},{3,7},{... | collective-permute-start | bytes 147464 | tf_op jit(solution)/shard_map/ppermute | solution.py:20
  42.3 4.1 %collective-permute-done.7 = bf16[2,6,4,4,1,1,128]{6,3,2,1,0,5,4:T(4,128)(2,1)S(1)} collective-permute-done((bf16[2,6,4,4,1,1,128]{6,3,2,1,0,5,4:T(4,128)(2,1)S(1)}, bf16[2,6,4,4,1,1,128]{6,3,2,1,0,5,4:T(4,128)(2,1)S(1)}, u32[]{:S(2)}, u32[]{:S(2)}) %collective-permute-start.7) | collective-permute-done | bytes 49184 | tf_op jit(solution)/shard_map/ppermute | solution.py:21
  48.7 4.7 %collective-permute-start.10 = (bf16[2,6,4,4,1,1,128]{6,3,2,1,0,5,4:T(4,128)(2,1)S(1)}, bf16[2,6,4,4,1,1,128]{6,3,2,1,0,5,4:T(4,128)(2,1)S(1)}, u32[]{:S(2)}, u32[]{:S(2)}) collective-permute-start(bf16[2,6,4,4,1,1,128]{6,3,2,1,0,5,4:T(4,128)(2,1)S(1)} %get-tuple-element.175), channel_id=1, source_target_pairs={{0,4},{4,8},{8,12},{1,5},{5,9},{9,13},{2,6},{6,10},{10,14},{3,7},{... | collective-permute-start | bytes 147464 | tf_op jit(solution)/shard_map/ppermute | solution.py:20
  54.7 4.5 %collective-permute-start.8 = (bf16[2,6,4,4,1,1,128]{6,3,2,1,0,5,4:T(4,128)(2,1)S(1)}, bf16[2,6,4,4,1,1,128]{6,3,2,1,0,5,4:T(4,128)(2,1)S(1)}, u32[]{:S(2)}, u32[]{:S(2)}) collective-permute-start(bf16[2,6,4,4,1,1,128]{6,3,2,1,0,5,4:T(4,128)(2,1)S(1)} %get-tuple-element.177), channel_id=1, source_target_pairs={{0,16},{1,17},{2,18},{3,19},{4,20},{5,21},{6,22},{7,23},{8,24},{9,... | collective-permute-start | bytes 147464 | tf_op jit(solution)/shard_map/ppermute | solution.py:20
  59.3 1.3 collective-permute-start.9
  61.2 4.4 %collective-permute-done.9 = bf16[2,6,4,4,1,1,128]{6,3,2,1,0,5,4:T(4,128)(2,1)S(1)} collective-permute-done((bf16[2,6,4,4,1,1,128]{6,3,2,1,0,5,4:T(4,128)(2,1)S(1)}, bf16[2,6,4,4,1,1,128]{6,3,2,1,0,5,4:T(4,128)(2,1)S(1)}, u32[]{:S(2)}, u32[]{:S(2)}) %collective-permute-start.9) | collective-permute-done | bytes 49184 | tf_op jit(solution)/shard_map/ppermute | solution.py:21
  71.2 2.1 collective-permute-start.12
  75.3 4.8 %scatter_custom_fusion.1 = f32[6144]{0:T(1024)S(1)} fusion(s32[768]{0:T(1024)} %copy-done.12, f32[768]{0:T(1024)S(1)} %fusion.5, f32[]{:T(128)} %constant.129.clone.1), kind=kCustom, calls=%fused_computation.296 | custom fusion | flops 768 | bytes 25088 | tf_op jit(solution)/shard_map/scatter-add | solution.py:181
  80.0 23.1 %psum.14 = f32[1,16,384]{2,0,1:T(1,128)} all-reduce(f32[1,16,384]{2,0,1:T(1,128)S(1)} %bitcast.739), channel_id=1, replica_groups=mesh['fx'=2,'fy'=4,'st'=4] {'fx','fy'}, use_global_device_ids=true, to_apply=%region_20.27 | all-reduce | flops 6144 | bytes 49152 | tf_op jit(solution)/shard_map/psum | solution.py:183
  103.2 3.9 %all-to-all-start.1 = ((f32[1,16,384]{2,0,1:T(1,128)}), f32[1,16,384]{2,0,1:T(1,128)}, u32[]{:S(2)}, u32[]{:S(2)}) async-start(f32[1,16,384]{2,0,1:T(1,128)} %psum.14), calls=%async_computation.1 | async-start | bytes 49152 | tf_op jit(solution)/shard_map/all_to_all | solution.py:184
  115.4 1.5 fusion.3
  117.6 5.1 %all-to-all-start.2 = ((bf16[4,4,384]{2,1,0:T(4,128)(2,1)}), bf16[4,4,384]{2,1,0:T(4,128)(2,1)S(1)}, u32[]{:S(2)}, u32[]{:S(2)}) async-start(bf16[4,4,384]{2,1,0:T(4,128)(2,1)} %copy.301), calls=%async_computation.2 | async-start | bytes 24576 | tf_op jit(solution)/shard_map/all_to_all | solution.py:155
  123.9 4.4 %all-to-all-done.2 = bf16[4,4,384]{2,1,0:T(4,128)(2,1)S(1)} async-done(((bf16[4,4,384]{2,1,0:T(4,128)(2,1)}), bf16[4,4,384]{2,1,0:T(4,128)(2,1)S(1)}, u32[]{:S(2)}, u32[]{:S(2)}) %all-to-all-start.2) | async-done | bytes 12320 | tf_op jit(solution)/shard_map/all_to_all | solution.py:155
  128.3 5.0 %gather_fusion.2 = bf16[768]{0:T(1024)(128)(2,1)S(1)} fusion(bf16[6144]{0:T(1024)(128)(2,1)S(1)} %reshape.2612, s32[1024]{0:T(1024)S(1)} %pad_clamp_fusion.1), kind=kCustom, calls=%fused_computation.2 | custom fusion | bytes 6144 | tf_op jit(solution)/shard_map/gather | solution.py:158
  133.6 1.5 scatter_custom_fusion.2
  137.1 4.5 %collective-permute-start.16 = (bf16[2,6,4,4,1,1,128]{6,3,2,1,0,5,4:T(4,128)(2,1)S(1)}, bf16[2,6,4,4,1,1,128]{6,3,2,1,0,5,4:T(4,128)(2,1)S(1)}, u32[]{:S(2)}, u32[]{:S(2)}) collective-permute-start(bf16[2,6,4,4,1,1,128]{6,3,2,1,0,5,4:T(4,128)(2,1)S(1)} %get-tuple-element.157), channel_id=1, source_target_pairs={{0,16},{1,17},{2,18},{3,19},{4,20},{5,21},{6,22},{7,23},{8,24},{9,... | collective-permute-start | bytes 147464 | tf_op jit(solution)/shard_map/ppermute | solution.py:20
  141.7 1.3 collective-permute-start.17
  143.0 1.3 collective-permute-start.18
  145.7 1.9 collective-permute-done.17
  147.6 1.9 collective-permute-done.19
  151.2 4.5 %collective-permute-start.20 = (bf16[2,6,4,4,1,1,128]{6,3,2,1,0,5,4:T(4,128)(2,1)S(1)}, bf16[2,6,4,4,1,1,128]{6,3,2,1,0,5,4:T(4,128)(2,1)S(1)}, u32[]{:S(2)}, u32[]{:S(2)}) collective-permute-start(bf16[2,6,4,4,1,1,128]{6,3,2,1,0,5,4:T(4,128)(2,1)S(1)} %get-tuple-element.147), channel_id=1, source_target_pairs={{0,16},{1,17},{2,18},{3,19},{4,20},{5,21},{6,22},{7,23},{8,24},{9,... | collective-permute-start | bytes 147464 | tf_op jit(solution)/shard_map/ppermute | solution.py:20
  157.0 4.4 %collective-permute-start.22 = (bf16[2,6,4,4,1,1,128]{6,3,2,1,0,5,4:T(4,128)(2,1)S(1)}, bf16[2,6,4,4,1,1,128]{6,3,2,1,0,5,4:T(4,128)(2,1)S(1)}, u32[]{:S(2)}, u32[]{:S(2)}) collective-permute-start(bf16[2,6,4,4,1,1,128]{6,3,2,1,0,5,4:T(4,128)(2,1)S(1)} %get-tuple-element.145), channel_id=1, source_target_pairs={{0,4},{4,8},{8,12},{1,5},{5,9},{9,13},{2,6},{6,10},{10,14},{3,7},{... | collective-permute-start | bytes 147464 | tf_op jit(solution)/shard_map/ppermute | solution.py:20
  167.3 4.8 %scatter_custom_fusion.3 = f32[6144]{0:T(1024)S(1)} fusion(s32[768]{0:T(1024)} %copy-done.12, f32[768]{0:T(1024)S(1)} %fusion.4, f32[]{:T(128)} %constant.129.clone.1), kind=kCustom, calls=%fused_computation.294 | custom fusion | flops 768 | bytes 25088 | tf_op jit(solution)/shard_map/scatter-add | solution.py:181
  172.0 25.3 %psum.15 = f32[1,16,384]{2,0,1:T(1,128)S(1)} all-reduce(f32[1,16,384]{2,0,1:T(1,128)S(1)} %bitcast.738), channel_id=1, replica_groups=mesh['fx'=2,'fy'=4,'st'=4] {'fx','fy'}, use_global_device_ids=true, to_apply=%region_41.48 | all-reduce | flops 6144 | bytes 49152 | tf_op jit(solution)/shard_map/psum | solution.py:183
  197.3 8.0 %all_to_all.42 = f32[1,16,384]{2,0,1:T(1,128)S(1)} all-to-all(f32[1,16,384]{2,0,1:T(1,128)S(1)} %psum.15), channel_id=1, replica_groups=mesh['fx'=2,'fy'=4,'st'=4] {'st'}, dimensions={1} | all-to-all | bytes 49152 | tf_op jit(solution)/shard_map/all_to_all | solution.py:184
  (256 shorter events, 49.9 us)
Async XLA Ops:
  0.6 10.0 %copy-start = (bf16[4,384,384]{2,1,0:T(8,128)(2,1)S(1)}, bf16[4,384,384]{2,1,0:T(8,128)(2,1)}, u32[]{:S(2)}) copy-start(bf16[4,384,384]{2,1,0:T(8,128)(2,1)} %param.33) | copy-start | bytes 3538948
  0.6 16.1 %copy-start.1 = (bf16[3,64,64]{2,1,0:T(8,128)(2,1)S(1)}, bf16[3,64,64]{2,1,0:T(8,128)(2,1)}, u32[]{:S(2)}) copy-start(bf16[3,64,64]{2,1,0:T(8,128)(2,1)} %param.29) | copy-start | bytes 73732
  0.7 28.4 %collective-permute-start = (bf16[2,6,4,4,1,1,128]{6,3,2,1,0,5,4:T(4,128)(2,1)S(1)}, bf16[2,6,4,4,1,1,128]{6,3,2,1,0,5,4:T(4,128)(2,1)S(1)}, u32[]{:S(2)}, u32[]{:S(2)}) collective-permute-start(bf16[2,6,4,4,1,1,128]{6,3,2,1,0,5,4:T(4,128)(2,1)S(1)} %get-tuple-element.197), channel_id=1, source_target_pairs={{0,16},{1,17},{2,18},{3,19},{4,20},{5,21},{6,22},{7,23},{8,24},{9,... | collective-permute-start | bytes 147464 | tf_op jit(solution)/shard_map/ppermute | solution.py:20
  5.8 23.3 %collective-permute-start.1 = (bf16[2,6,4,4,1,1,128]{6,3,2,1,0,5,4:T(4,128)(2,1)S(1)}, bf16[2,6,4,4,1,1,128]{6,3,2,1,0,5,4:T(4,128)(2,1)S(1)}, u32[]{:S(2)}, u32[]{:S(2)}) collective-permute-start(bf16[2,6,4,4,1,1,128]{6,3,2,1,0,5,4:T(4,128)(2,1)S(1)} %get-tuple-element.198), channel_id=1, source_target_pairs={{16,0},{17,1},{18,2},{19,3},{20,4},{21,5},{22,6},{23,7},{24,8},{25... | collective-permute-start | bytes 147464 | tf_op jit(solution)/shard_map/ppermute | solution.py:21
  7.1 22.0 %collective-permute-start.2 = (bf16[2,6,4,4,1,1,128]{6,3,2,1,0,5,4:T(4,128)(2,1)S(1)}, bf16[2,6,4,4,1,1,128]{6,3,2,1,0,5,4:T(4,128)(2,1)S(1)}, u32[]{:S(2)}, u32[]{:S(2)}) collective-permute-start(bf16[2,6,4,4,1,1,128]{6,3,2,1,0,5,4:T(4,128)(2,1)S(1)} %get-tuple-element.195), channel_id=1, source_target_pairs={{0,4},{4,8},{8,12},{1,5},{5,9},{9,13},{2,6},{6,10},{10,14},{3,7},{... | collective-permute-start | bytes 147464 | tf_op jit(solution)/shard_map/ppermute | solution.py:20
  8.6 20.5 %collective-permute-start.3 = (bf16[2,6,4,4,1,1,128]{6,3,2,1,0,5,4:T(4,128)(2,1)S(1)}, bf16[2,6,4,4,1,1,128]{6,3,2,1,0,5,4:T(4,128)(2,1)S(1)}, u32[]{:S(2)}, u32[]{:S(2)}) collective-permute-start(bf16[2,6,4,4,1,1,128]{6,3,2,1,0,5,4:T(4,128)(2,1)S(1)} %get-tuple-element.196), channel_id=1, source_target_pairs={{4,0},{8,4},{12,8},{5,1},{9,5},{13,9},{6,2},{10,6},{14,10},{7,3},{... | collective-permute-start | bytes 147464 | tf_op jit(solution)/shard_map/ppermute | solution.py:21
  11.7 10.5 %all-to-all-start = ((bf16[4,4,384]{2,1,0:T(4,128)(2,1)}), bf16[4,4,384]{2,1,0:T(4,128)(2,1)S(1)}, u32[]{:S(2)}, u32[]{:S(2)}) async-start(bf16[4,4,384]{2,1,0:T(4,128)(2,1)} %copy.260), calls=%async_computation | async-start | bytes 24576 | tf_op jit(solution)/shard_map/all_to_all | solution.py:155
  31.5 10.2 %collective-permute-start.4 = (bf16[2,6,4,4,1,1,128]{6,3,2,1,0,5,4:T(4,128)(2,1)S(1)}, bf16[2,6,4,4,1,1,128]{6,3,2,1,0,5,4:T(4,128)(2,1)S(1)}, u32[]{:S(2)}, u32[]{:S(2)}) collective-permute-start(bf16[2,6,4,4,1,1,128]{6,3,2,1,0,5,4:T(4,128)(2,1)S(1)} %get-tuple-element.187), channel_id=1, source_target_pairs={{0,16},{1,17},{2,18},{3,19},{4,20},{5,21},{6,22},{7,23},{8,24},{9,... | collective-permute-start | bytes 147464 | tf_op jit(solution)/shard_map/ppermute | solution.py:20
  35.9 6.3 %collective-permute-start.5 = (bf16[2,6,4,4,1,1,128]{6,3,2,1,0,5,4:T(4,128)(2,1)S(1)}, bf16[2,6,4,4,1,1,128]{6,3,2,1,0,5,4:T(4,128)(2,1)S(1)}, u32[]{:S(2)}, u32[]{:S(2)}) collective-permute-start(bf16[2,6,4,4,1,1,128]{6,3,2,1,0,5,4:T(4,128)(2,1)S(1)} %get-tuple-element.188), channel_id=1, source_target_pairs={{16,0},{17,1},{18,2},{19,3},{20,4},{21,5},{22,6},{23,7},{24,8},{25... | collective-permute-start | bytes 147464 | tf_op jit(solution)/shard_map/ppermute | solution.py:21
  37.2 5.0 %collective-permute-start.6 = (bf16[2,6,4,4,1,1,128]{6,3,2,1,0,5,4:T(4,128)(2,1)S(1)}, bf16[2,6,4,4,1,1,128]{6,3,2,1,0,5,4:T(4,128)(2,1)S(1)}, u32[]{:S(2)}, u32[]{:S(2)}) collective-permute-start(bf16[2,6,4,4,1,1,128]{6,3,2,1,0,5,4:T(4,128)(2,1)S(1)} %get-tuple-element.185), channel_id=1, source_target_pairs={{0,4},{4,8},{8,12},{1,5},{5,9},{9,13},{2,6},{6,10},{10,14},{3,7},{... | collective-permute-start | bytes 147464 | tf_op jit(solution)/shard_map/ppermute | solution.py:20
  40.3 6.1 %collective-permute-start.7 = (bf16[2,6,4,4,1,1,128]{6,3,2,1,0,5,4:T(4,128)(2,1)S(1)}, bf16[2,6,4,4,1,1,128]{6,3,2,1,0,5,4:T(4,128)(2,1)S(1)}, u32[]{:S(2)}, u32[]{:S(2)}) collective-permute-start(bf16[2,6,4,4,1,1,128]{6,3,2,1,0,5,4:T(4,128)(2,1)S(1)} %get-tuple-element.186), channel_id=1, source_target_pairs={{4,0},{8,4},{12,8},{5,1},{9,5},{13,9},{6,2},{10,6},{14,10},{7,3},{... | collective-permute-start | bytes 147464 | tf_op jit(solution)/shard_map/ppermute | solution.py:21
  48.7 12.0 %collective-permute-start.10 = (bf16[2,6,4,4,1,1,128]{6,3,2,1,0,5,4:T(4,128)(2,1)S(1)}, bf16[2,6,4,4,1,1,128]{6,3,2,1,0,5,4:T(4,128)(2,1)S(1)}, u32[]{:S(2)}, u32[]{:S(2)}) collective-permute-start(bf16[2,6,4,4,1,1,128]{6,3,2,1,0,5,4:T(4,128)(2,1)S(1)} %get-tuple-element.175), channel_id=1, source_target_pairs={{0,4},{4,8},{8,12},{1,5},{5,9},{9,13},{2,6},{6,10},{10,14},{3,7},{... | collective-permute-start | bytes 147464 | tf_op jit(solution)/shard_map/ppermute | solution.py:20
  53.4 7.3 %collective-permute-start.11 = (bf16[2,6,4,4,1,1,128]{6,3,2,1,0,5,4:T(4,128)(2,1)S(1)}, bf16[2,6,4,4,1,1,128]{6,3,2,1,0,5,4:T(4,128)(2,1)S(1)}, u32[]{:S(2)}, u32[]{:S(2)}) collective-permute-start(bf16[2,6,4,4,1,1,128]{6,3,2,1,0,5,4:T(4,128)(2,1)S(1)} %get-tuple-element.176), channel_id=1, source_target_pairs={{4,0},{8,4},{12,8},{5,1},{9,5},{13,9},{6,2},{10,6},{14,10},{7,3},{... | collective-permute-start | bytes 147464 | tf_op jit(solution)/shard_map/ppermute | solution.py:21
  54.7 6.5 %collective-permute-start.8 = (bf16[2,6,4,4,1,1,128]{6,3,2,1,0,5,4:T(4,128)(2,1)S(1)}, bf16[2,6,4,4,1,1,128]{6,3,2,1,0,5,4:T(4,128)(2,1)S(1)}, u32[]{:S(2)}, u32[]{:S(2)}) collective-permute-start(bf16[2,6,4,4,1,1,128]{6,3,2,1,0,5,4:T(4,128)(2,1)S(1)} %get-tuple-element.177), channel_id=1, source_target_pairs={{0,16},{1,17},{2,18},{3,19},{4,20},{5,21},{6,22},{7,23},{8,24},{9,... | collective-permute-start | bytes 147464 | tf_op jit(solution)/shard_map/ppermute | solution.py:20
  59.3 6.4 %collective-permute-start.9 = (bf16[2,6,4,4,1,1,128]{6,3,2,1,0,5,4:T(4,128)(2,1)S(1)}, bf16[2,6,4,4,1,1,128]{6,3,2,1,0,5,4:T(4,128)(2,1)S(1)}, u32[]{:S(2)}, u32[]{:S(2)}) collective-permute-start(bf16[2,6,4,4,1,1,128]{6,3,2,1,0,5,4:T(4,128)(2,1)S(1)} %get-tuple-element.178), channel_id=1, source_target_pairs={{16,0},{17,1},{18,2},{19,3},{20,4},{21,5},{22,6},{23,7},{24,8},{25... | collective-permute-start | bytes 147464 | tf_op jit(solution)/shard_map/ppermute | solution.py:21
  71.2 51.5 %collective-permute-start.12 = (bf16[2,6,4,4,1,1,128]{6,3,2,1,0,5,4:T(4,128)(2,1)}, bf16[2,6,4,4,1,1,128]{6,3,2,1,0,5,4:T(4,128)(2,1)}, u32[]{:S(2)}, u32[]{:S(2)}) collective-permute-start(bf16[2,6,4,4,1,1,128]{6,3,2,1,0,5,4:T(4,128)(2,1)} %get-tuple-element.167), channel_id=1, source_target_pairs={{0,16},{1,17},{2,18},{3,19},{4,20},{5,21},{6,22},{7,23},{8,24},{9,... | collective-permute-start | bytes 147464 | tf_op jit(solution)/shard_map/ppermute | solution.py:20
  73.3 34.7 %copy-start.2 = (f32[6,64,128]{2,1,0:T(8,128)S(1)}, f32[6,64,128]{2,1,0:T(8,128)}, u32[]{:S(2)}) copy-start(f32[6,64,128]{2,1,0:T(8,128)} %multiply_reduce_fusion.12) | copy-start | bytes 589828
  103.2 10.7 %all-to-all-start.1 = ((f32[1,16,384]{2,0,1:T(1,128)}), f32[1,16,384]{2,0,1:T(1,128)}, u32[]{:S(2)}, u32[]{:S(2)}) async-start(f32[1,16,384]{2,0,1:T(1,128)} %psum.14), calls=%async_computation.1 | async-start | bytes 49152 | tf_op jit(solution)/shard_map/all_to_all | solution.py:184
  110.0 12.7 %collective-permute-start.13 = (bf16[2,6,4,4,1,1,128]{6,3,2,1,0,5,4:T(4,128)(2,1)}, bf16[2,6,4,4,1,1,128]{6,3,2,1,0,5,4:T(4,128)(2,1)S(1)}, u32[]{:S(2)}, u32[]{:S(2)}) collective-permute-start(bf16[2,6,4,4,1,1,128]{6,3,2,1,0,5,4:T(4,128)(2,1)} %get-tuple-element.168), channel_id=1, source_target_pairs={{16,0},{17,1},{18,2},{19,3},{20,4},{21,5},{22,6},{23,7},{24,8},{25... | collective-permute-start | bytes 147464 | tf_op jit(solution)/shard_map/ppermute | solution.py:21
  111.3 11.4 %collective-permute-start.14 = (bf16[2,6,4,4,1,1,128]{6,3,2,1,0,5,4:T(4,128)(2,1)}, bf16[2,6,4,4,1,1,128]{6,3,2,1,0,5,4:T(4,128)(2,1)S(1)}, u32[]{:S(2)}, u32[]{:S(2)}) collective-permute-start(bf16[2,6,4,4,1,1,128]{6,3,2,1,0,5,4:T(4,128)(2,1)} %get-tuple-element.165), channel_id=1, source_target_pairs={{0,4},{4,8},{8,12},{1,5},{5,9},{9,13},{2,6},{6,10},{10,14},{3,7},{... | collective-permute-start | bytes 147464 | tf_op jit(solution)/shard_map/ppermute | solution.py:20
  112.6 10.1 %collective-permute-start.15 = (bf16[2,6,4,4,1,1,128]{6,3,2,1,0,5,4:T(4,128)(2,1)}, bf16[2,6,4,4,1,1,128]{6,3,2,1,0,5,4:T(4,128)(2,1)S(1)}, u32[]{:S(2)}, u32[]{:S(2)}) collective-permute-start(bf16[2,6,4,4,1,1,128]{6,3,2,1,0,5,4:T(4,128)(2,1)} %get-tuple-element.166), channel_id=1, source_target_pairs={{4,0},{8,4},{12,8},{5,1},{9,5},{13,9},{6,2},{10,6},{14,10},{7,3},{... | collective-permute-start | bytes 147464 | tf_op jit(solution)/shard_map/ppermute | solution.py:21
  117.6 10.7 %all-to-all-start.2 = ((bf16[4,4,384]{2,1,0:T(4,128)(2,1)}), bf16[4,4,384]{2,1,0:T(4,128)(2,1)S(1)}, u32[]{:S(2)}, u32[]{:S(2)}) async-start(bf16[4,4,384]{2,1,0:T(4,128)(2,1)} %copy.301), calls=%async_computation.2 | async-start | bytes 24576 | tf_op jit(solution)/shard_map/all_to_all | solution.py:155
  137.1 8.6 %collective-permute-start.16 = (bf16[2,6,4,4,1,1,128]{6,3,2,1,0,5,4:T(4,128)(2,1)S(1)}, bf16[2,6,4,4,1,1,128]{6,3,2,1,0,5,4:T(4,128)(2,1)S(1)}, u32[]{:S(2)}, u32[]{:S(2)}) collective-permute-start(bf16[2,6,4,4,1,1,128]{6,3,2,1,0,5,4:T(4,128)(2,1)S(1)} %get-tuple-element.157), channel_id=1, source_target_pairs={{0,16},{1,17},{2,18},{3,19},{4,20},{5,21},{6,22},{7,23},{8,24},{9,... | collective-permute-start | bytes 147464 | tf_op jit(solution)/shard_map/ppermute | solution.py:20
  141.7 6.0 %collective-permute-start.17 = (bf16[2,6,4,4,1,1,128]{6,3,2,1,0,5,4:T(4,128)(2,1)S(1)}, bf16[2,6,4,4,1,1,128]{6,3,2,1,0,5,4:T(4,128)(2,1)S(1)}, u32[]{:S(2)}, u32[]{:S(2)}) collective-permute-start(bf16[2,6,4,4,1,1,128]{6,3,2,1,0,5,4:T(4,128)(2,1)S(1)} %get-tuple-element.158), channel_id=1, source_target_pairs={{16,0},{17,1},{18,2},{19,3},{20,4},{21,5},{22,6},{23,7},{24,8},{25... | collective-permute-start | bytes 147464 | tf_op jit(solution)/shard_map/ppermute | solution.py:21
  143.0 4.7 %collective-permute-start.18 = (bf16[2,6,4,4,1,1,128]{6,3,2,1,0,5,4:T(4,128)(2,1)S(1)}, bf16[2,6,4,4,1,1,128]{6,3,2,1,0,5,4:T(4,128)(2,1)S(1)}, u32[]{:S(2)}, u32[]{:S(2)}) collective-permute-start(bf16[2,6,4,4,1,1,128]{6,3,2,1,0,5,4:T(4,128)(2,1)S(1)} %get-tuple-element.155), channel_id=1, source_target_pairs={{0,4},{4,8},{8,12},{1,5},{5,9},{9,13},{2,6},{6,10},{10,14},{3,7},{... | collective-permute-start | bytes 147464 | tf_op jit(solution)/shard_map/ppermute | solution.py:20
  144.3 5.3 %collective-permute-start.19 = (bf16[2,6,4,4,1,1,128]{6,3,2,1,0,5,4:T(4,128)(2,1)S(1)}, bf16[2,6,4,4,1,1,128]{6,3,2,1,0,5,4:T(4,128)(2,1)S(1)}, u32[]{:S(2)}, u32[]{:S(2)}) collective-permute-start(bf16[2,6,4,4,1,1,128]{6,3,2,1,0,5,4:T(4,128)(2,1)S(1)} %get-tuple-element.156), channel_id=1, source_target_pairs={{4,0},{8,4},{12,8},{5,1},{9,5},{13,9},{6,2},{10,6},{14,10},{7,3},{... | collective-permute-start | bytes 147464 | tf_op jit(solution)/shard_map/ppermute | solution.py:21
  151.2 12.3 %collective-permute-start.20 = (bf16[2,6,4,4,1,1,128]{6,3,2,1,0,5,4:T(4,128)(2,1)S(1)}, bf16[2,6,4,4,1,1,128]{6,3,2,1,0,5,4:T(4,128)(2,1)S(1)}, u32[]{:S(2)}, u32[]{:S(2)}) collective-permute-start(bf16[2,6,4,4,1,1,128]{6,3,2,1,0,5,4:T(4,128)(2,1)S(1)} %get-tuple-element.147), channel_id=1, source_target_pairs={{0,16},{1,17},{2,18},{3,19},{4,20},{5,21},{6,22},{7,23},{8,24},{9,... | collective-permute-start | bytes 147464 | tf_op jit(solution)/shard_map/ppermute | solution.py:20
  155.7 7.8 %collective-permute-start.21 = (bf16[2,6,4,4,1,1,128]{6,3,2,1,0,5,4:T(4,128)(2,1)S(1)}, bf16[2,6,4,4,1,1,128]{6,3,2,1,0,5,4:T(4,128)(2,1)S(1)}, u32[]{:S(2)}, u32[]{:S(2)}) collective-permute-start(bf16[2,6,4,4,1,1,128]{6,3,2,1,0,5,4:T(4,128)(2,1)S(1)} %get-tuple-element.148), channel_id=1, source_target_pairs={{16,0},{17,1},{18,2},{19,3},{20,4},{21,5},{22,6},{23,7},{24,8},{25... | collective-permute-start | bytes 147464 | tf_op jit(solution)/shard_map/ppermute | solution.py:21
  157.0 6.5 %collective-permute-start.22 = (bf16[2,6,4,4,1,1,128]{6,3,2,1,0,5,4:T(4,128)(2,1)S(1)}, bf16[2,6,4,4,1,1,128]{6,3,2,1,0,5,4:T(4,128)(2,1)S(1)}, u32[]{:S(2)}, u32[]{:S(2)}) collective-permute-start(bf16[2,6,4,4,1,1,128]{6,3,2,1,0,5,4:T(4,128)(2,1)S(1)} %get-tuple-element.145), channel_id=1, source_target_pairs={{0,4},{4,8},{8,12},{1,5},{5,9},{9,13},{2,6},{6,10},{10,14},{3,7},{... | collective-permute-start | bytes 147464 | tf_op jit(solution)/shard_map/ppermute | solution.py:20
  161.4 3.1 %collective-permute-start.23 = (bf16[2,6,4,4,1,1,128]{6,3,2,1,0,5,4:T(4,128)(2,1)S(1)}, bf16[2,6,4,4,1,1,128]{6,3,2,1,0,5,4:T(4,128)(2,1)S(1)}, u32[]{:S(2)}, u32[]{:S(2)}) collective-permute-start(bf16[2,6,4,4,1,1,128]{6,3,2,1,0,5,4:T(4,128)(2,1)S(1)} %get-tuple-element.146), channel_id=1, source_target_pairs={{4,0},{8,4},{12,8},{5,1},{9,5},{13,9},{6,2},{10,6},{14,10},{7,3},{... | collective-permute-start | bytes 147464 | tf_op jit(solution)/shard_map/ppermute | solution.py:21
  165.1 40.2 %copy-start.8 = (f32[4,4,384]{2,1,0:T(4,128)S(1)}, f32[4,4,384]{2,1,0:T(4,128)}, u32[]{:S(2)}) copy-start(f32[4,4,384]{2,1,0:T(4,128)} %param.35) | copy-start | bytes 73732
  166.0 39.8 %copy-start.6 = (f32[4,4,384]{2,1,0:T(4,128)S(1)}, f32[4,4,384]{2,1,0:T(4,128)}, u32[]{:S(2)}) copy-start(f32[4,4,384]{2,1,0:T(4,128)} %param.34) | copy-start | bytes 73732
  (15 other events, 68.7 us)
where the time goes:
time: 209 us; the launch traced here: 208 us
  starting transfers between devices  70.7 us (34%)
  blocking collectives  56.4 us (27%)
  other arithmetic  28.5 us (14%)
  local copies, waits for them, and re-layouts  21.8 us (10%)
  waiting for transfers between devices  20 us (10%)
  matrix products  7.17 us (3%)
  between operations  2.87 us (1%)
    psum x2, blocking collectives, body(): summed = lax.psum(partial_loads, ('fx', 'fy'))  48.4 us
    ppermute x12, starting transfers between devices, with_halo(): before = lax.ppermute(last, axis, up)  41.3 us
    ppermute x12, starting transfers between devices, with_halo(): after = lax.ppermute(initial, axis, down)  15.5 us
    ppermute x12, waiting for transfers between devices, with_halo(): after = lax.ppermute(initial, axis, down)  13.9 us
    gather x2, local copies, waits for them, and re-layouts, body(): picked = received.reshape(-1)[columns]  10 us
    all_to_all x2, starting transfers between devices, body(): lax.all_to_all(shell_tangent.astype(jnp.bfloat16), 'st', split_axis=0, co...  9.96 us
    scatter-add x2, other arithmetic, body(): jnp.zeros((panels * SDOF * PN,), jnp.float32).at[columns].add(loads)  9.5 us
    all_to_all x1, blocking collectives, body(): lax.all_to_all(summed, 'st', split_axis=1, concat_axis=0, tiled=True)  7.97 us
  transfers between devices with their start and end apart: 27, of which 9 were waited for; matrix products, arithmetic and copies ran while one was open for 13% of the time, Pallas kernels for 0%

commit v1 on v0

--- a/solution.py
+++ b/solution.py
@@ -180,7 +180,7 @@
         panels = received.shape[1]
         partial_loads = jnp.zeros((panels * SDOF * PN,), jnp.float32).at[columns].add(loads)
         partial_loads = partial_loads.reshape(1, panels, SDOF * PN)
-        summed = lax.psum(partial_loads, ("fx", "fy"))
+        summed = jnp.sum(lax.all_gather(partial_loads, ("fx", "fy")), axis=0)
         owned = lax.all_to_all(summed, "st", split_axis=1, concat_axis=0, tiled=True)
         shell_adjoint = shell_solve(shell_adjoint_rhs - owned)
         shell_tangent = shell_solve(shell_load + shell_adjoint)

time: 209 us -> 181 us (0.87)
  blocking collectives: 56.4 us -> 28.9 us
    psum x2 -> x0, blocking collectives: 48.4 us -> none  [body(): summed = lax.psum(partial_loads, ('fx', 'fy'))]
    all_gather x0 -> x2, blocking collectives: none -> 20.9 us  [body(): summed = jnp.sum(lax.all_gather(partial_loads, ('fx', 'fy')), axis=0)]
  transfers between devices with their start and end apart: 27 -> 27, of which waited for: 9 -> 9; matrix products, arithmetic and copies ran while one was open for 13% -> 14% of each run, Pallas kernels for 0% -> 0%
where the time goes in v1:
time: 181 us; the launch traced here: 180 us
  starting transfers between devices  71 us (39%)
  blocking collectives  28.9 us (16%)
  other arithmetic  26.9 us (15%)
  local copies, waits for them, and re-layouts  22.1 us (12%)
  waiting for transfers between devices  21.2 us (12%)
  matrix products  6.55 us (4%)
  between operations  2.98 us (2%)
    ppermute x12, starting transfers between devices, with_halo(): before = lax.ppermute(last, axis, up)  42 us
    all_gather x2, blocking collectives, body(): summed = jnp.sum(lax.all_gather(partial_loads, ('fx', 'fy')), axis=0)  20.9 us
    ppermute x12, starting transfers between devices, with_halo(): after = lax.ppermute(initial, axis, down)  15.5 us
    ppermute x12, waiting for transfers between devices, with_halo(): after = lax.ppermute(initial, axis, down)  14.6 us
    gather x2, local copies, waits for them, and re-layouts, body(): picked = received.reshape(-1)[columns]  10 us
    all_to_all x2, starting transfers between devices, body(): lax.all_to_all(shell_tangent.astype(jnp.bfloat16), 'st', split_axis=0, co...  9.62 us
    scatter-add x2, other arithmetic, body(): jnp.zeros((panels * SDOF * PN,), jnp.float32).at[columns].add(loads)  9.5 us
    all_to_all x1, blocking collectives, body(): lax.all_to_all(summed, 'st', split_axis=1, concat_axis=0, tiled=True)  7.99 us
  transfers between devices with their start and end apart: 27, of which 9 were waited for; matrix products, arithmetic and copies ran while one was open for 14% of the time, Pallas kernels for 0%

profile of v1, /device:TPU:0, one launch (start us, length us, event | category | flops | bytes accessed | tf_op | source)
XLA Modules:
  0.0 179.7 jit_solution(4400535876023862956)
XLA Ops:
  0.7 5.0 %collective-permute-start = (bf16[2,6,4,4,1,1,128]{6,3,2,1,0,5,4:T(4,128)(2,1)S(1)}, bf16[2,6,4,4,1,1,128]{6,3,2,1,0,5,4:T(4,128)(2,1)S(1)}, u32[]{:S(2)}, u32[]{:S(2)}) collective-permute-start(bf16[2,6,4,4,1,1,128]{6,3,2,1,0,5,4:T(4,128)(2,1)S(1)} %get-tuple-element.197), channel_id=1, source_target_pairs={{0,16},{1,17},{2,18},{3,19},{4,20},{5,21},{6,22},{7,23},{8,24},{9,... | collective-permute-start | bytes 147464 | tf_op jit(solution)/shard_map/ppermute | solution.py:20
  5.8 1.3 collective-permute-start.1
  7.1 1.5 collective-permute-start.2
  11.7 4.9 %all-to-all-start = ((bf16[4,4,384]{2,1,0:T(4,128)(2,1)}), bf16[4,4,384]{2,1,0:T(4,128)(2,1)S(1)}, u32[]{:S(2)}, u32[]{:S(2)}) async-start(bf16[4,4,384]{2,1,0:T(4,128)(2,1)} %copy.260), calls=%async_computation | async-start | bytes 24576 | tf_op jit(solution)/shard_map/all_to_all | solution.py:155
  20.4 1.8 all-to-all-done
  22.2 5.0 %gather_fusion = bf16[768]{0:T(1024)(128)(2,1)S(1)} fusion(bf16[6144]{0:T(1024)(128)(2,1)S(1)} %reshape.2595, s32[1024]{0:T(1024)S(1)} %pad_clamp_fusion.1), kind=kCustom, calls=%fused_computation | custom fusion | bytes 6144 | tf_op jit(solution)/shard_map/gather | solution.py:158
  27.5 1.4 scatter_custom_fusion
  31.5 4.4 %collective-permute-start.4 = (bf16[2,6,4,4,1,1,128]{6,3,2,1,0,5,4:T(4,128)(2,1)S(1)}, bf16[2,6,4,4,1,1,128]{6,3,2,1,0,5,4:T(4,128)(2,1)S(1)}, u32[]{:S(2)}, u32[]{:S(2)}) collective-permute-start(bf16[2,6,4,4,1,1,128]{6,3,2,1,0,5,4:T(4,128)(2,1)S(1)} %get-tuple-element.187), channel_id=1, source_target_pairs={{0,16},{1,17},{2,18},{3,19},{4,20},{5,21},{6,22},{7,23},{8,24},{9,... | collective-permute-start | bytes 147464 | tf_op jit(solution)/shard_map/ppermute | solution.py:20
  37.2 3.0 %collective-permute-start.6 = (bf16[2,6,4,4,1,1,128]{6,3,2,1,0,5,4:T(4,128)(2,1)S(1)}, bf16[2,6,4,4,1,1,128]{6,3,2,1,0,5,4:T(4,128)(2,1)S(1)}, u32[]{:S(2)}, u32[]{:S(2)}) collective-permute-start(bf16[2,6,4,4,1,1,128]{6,3,2,1,0,5,4:T(4,128)(2,1)S(1)} %get-tuple-element.185), channel_id=1, source_target_pairs={{0,4},{4,8},{8,12},{1,5},{5,9},{9,13},{2,6},{6,10},{10,14},{3,7},{... | collective-permute-start | bytes 147464 | tf_op jit(solution)/shard_map/ppermute | solution.py:20
  42.3 4.1 %collective-permute-done.7 = bf16[2,6,4,4,1,1,128]{6,3,2,1,0,5,4:T(4,128)(2,1)S(1)} collective-permute-done((bf16[2,6,4,4,1,1,128]{6,3,2,1,0,5,4:T(4,128)(2,1)S(1)}, bf16[2,6,4,4,1,1,128]{6,3,2,1,0,5,4:T(4,128)(2,1)S(1)}, u32[]{:S(2)}, u32[]{:S(2)}) %collective-permute-start.7) | collective-permute-done | bytes 49184 | tf_op jit(solution)/shard_map/ppermute | solution.py:21
  48.7 4.7 %collective-permute-start.10 = (bf16[2,6,4,4,1,1,128]{6,3,2,1,0,5,4:T(4,128)(2,1)S(1)}, bf16[2,6,4,4,1,1,128]{6,3,2,1,0,5,4:T(4,128)(2,1)S(1)}, u32[]{:S(2)}, u32[]{:S(2)}) collective-permute-start(bf16[2,6,4,4,1,1,128]{6,3,2,1,0,5,4:T(4,128)(2,1)S(1)} %get-tuple-element.175), channel_id=1, source_target_pairs={{0,4},{4,8},{8,12},{1,5},{5,9},{9,13},{2,6},{6,10},{10,14},{3,7},{... | collective-permute-start | bytes 147464 | tf_op jit(solution)/shard_map/ppermute | solution.py:20
  54.7 4.5 %collective-permute-start.8 = (bf16[2,6,4,4,1,1,128]{6,3,2,1,0,5,4:T(4,128)(2,1)S(1)}, bf16[2,6,4,4,1,1,128]{6,3,2,1,0,5,4:T(4,128)(2,1)S(1)}, u32[]{:S(2)}, u32[]{:S(2)}) collective-permute-start(bf16[2,6,4,4,1,1,128]{6,3,2,1,0,5,4:T(4,128)(2,1)S(1)} %get-tuple-element.177), channel_id=1, source_target_pairs={{0,16},{1,17},{2,18},{3,19},{4,20},{5,21},{6,22},{7,23},{8,24},{9,... | collective-permute-start | bytes 147464 | tf_op jit(solution)/shard_map/ppermute | solution.py:20
  61.2 4.4 %collective-permute-done.9 = bf16[2,6,4,4,1,1,128]{6,3,2,1,0,5,4:T(4,128)(2,1)S(1)} collective-permute-done((bf16[2,6,4,4,1,1,128]{6,3,2,1,0,5,4:T(4,128)(2,1)S(1)}, bf16[2,6,4,4,1,1,128]{6,3,2,1,0,5,4:T(4,128)(2,1)S(1)}, u32[]{:S(2)}, u32[]{:S(2)}) %collective-permute-start.9) | collective-permute-done | bytes 49184 | tf_op jit(solution)/shard_map/ppermute | solution.py:21
  71.8 2.1 %collective-permute-start.12 = (bf16[2,6,4,4,1,1,128]{6,3,2,1,0,5,4:T(4,128)(2,1)}, bf16[2,6,4,4,1,1,128]{6,3,2,1,0,5,4:T(4,128)(2,1)}, u32[]{:S(2)}, u32[]{:S(2)}) collective-permute-start(bf16[2,6,4,4,1,1,128]{6,3,2,1,0,5,4:T(4,128)(2,1)} %get-tuple-element.167), channel_id=1, source_target_pairs={{0,16},{1,17},{2,18},{3,19},{4,20},{5,21},{6,22},{7,23},{8,24},{9,... | collective-permute-start | bytes 147464 | tf_op jit(solution)/shard_map/ppermute | solution.py:20
  75.0 4.8 %scatter_custom_fusion.1 = f32[6144]{0:T(1024)S(1)} fusion(s32[768]{0:T(1024)} %copy-done.16, f32[768]{0:T(1024)S(1)} %fusion.5, f32[]{:T(128)} %constant.129.clone.1), kind=kCustom, calls=%fused_computation.296 | custom fusion | flops 768 | bytes 25088 | tf_op jit(solution)/shard_map/scatter-add | solution.py:181
  79.8 9.9 %all_gather.6 = f32[8,1,16,384]{3,2,1,0:T(8,128)S(1)} all-gather(f32[1,1,16,384]{3,2,1,0:T(8,128)S(1)} %all_gather_reshape.6), channel_id=1, replica_groups=mesh['fx'=2,'fy'=4,'st'=4] {'fx','fy'}, dimensions={0}, use_global_device_ids=true | all-gather | bytes 221184 | tf_op jit(solution)/shard_map/all_gather | solution.py:183
  90.4 3.9 %all-to-all-start.1 = ((f32[1,16,384]{2,0,1:T(1,128)}), f32[1,16,384]{2,0,1:T(1,128)}, u32[]{:S(2)}, u32[]{:S(2)}) async-start(f32[1,16,384]{2,0,1:T(1,128)} %reduce_sum.365), calls=%async_computation.1 | async-start | bytes 49152 | tf_op jit(solution)/shard_map/all_to_all | solution.py:184
  96.7 2.3 %collective-permute-start.14 = (bf16[2,6,4,4,1,1,128]{6,3,2,1,0,5,4:T(4,128)(2,1)}, bf16[2,6,4,4,1,1,128]{6,3,2,1,0,5,4:T(4,128)(2,1)S(1)}, u32[]{:S(2)}, u32[]{:S(2)}) collective-permute-start(bf16[2,6,4,4,1,1,128]{6,3,2,1,0,5,4:T(4,128)(2,1)} %get-tuple-element.165), channel_id=1, source_target_pairs={{0,4},{4,8},{8,12},{1,5},{5,9},{9,13},{2,6},{6,10},{10,14},{3,7},{... | collective-permute-start | bytes 147464 | tf_op jit(solution)/shard_map/ppermute | solution.py:20
  101.8 1.5 fusion.3
  104.0 4.7 %all-to-all-start.2 = ((bf16[4,4,384]{2,1,0:T(4,128)(2,1)}), bf16[4,4,384]{2,1,0:T(4,128)(2,1)S(1)}, u32[]{:S(2)}, u32[]{:S(2)}) async-start(bf16[4,4,384]{2,1,0:T(4,128)(2,1)} %copy.301), calls=%async_computation.2 | async-start | bytes 24576 | tf_op jit(solution)/shard_map/all_to_all | solution.py:155
  110.0 4.4 %all-to-all-done.2 = bf16[4,4,384]{2,1,0:T(4,128)(2,1)S(1)} async-done(((bf16[4,4,384]{2,1,0:T(4,128)(2,1)}), bf16[4,4,384]{2,1,0:T(4,128)(2,1)S(1)}, u32[]{:S(2)}, u32[]{:S(2)}) %all-to-all-start.2) | async-done | bytes 12320 | tf_op jit(solution)/shard_map/all_to_all | solution.py:155
  114.4 5.0 %gather_fusion.2 = bf16[768]{0:T(1024)(128)(2,1)S(1)} fusion(bf16[6144]{0:T(1024)(128)(2,1)S(1)} %reshape.2607, s32[1024]{0:T(1024)S(1)} %pad_clamp_fusion.1), kind=kCustom, calls=%fused_computation.2 | custom fusion | bytes 6144 | tf_op jit(solution)/shard_map/gather | solution.py:158
  119.6 1.5 scatter_custom_fusion.2
  123.2 4.3 %collective-permute-start.16 = (bf16[2,6,4,4,1,1,128]{6,3,2,1,0,5,4:T(4,128)(2,1)S(1)}, bf16[2,6,4,4,1,1,128]{6,3,2,1,0,5,4:T(4,128)(2,1)S(1)}, u32[]{:S(2)}, u32[]{:S(2)}) collective-permute-start(bf16[2,6,4,4,1,1,128]{6,3,2,1,0,5,4:T(4,128)(2,1)S(1)} %get-tuple-element.157), channel_id=1, source_target_pairs={{0,16},{1,17},{2,18},{3,19},{4,20},{5,21},{6,22},{7,23},{8,24},{9,... | collective-permute-start | bytes 147464 | tf_op jit(solution)/shard_map/ppermute | solution.py:20
  128.8 1.3 collective-permute-start.18
  131.5 1.9 %collective-permute-done.17 = bf16[2,6,4,4,1,1,128]{6,3,2,1,0,5,4:T(4,128)(2,1)S(1)} collective-permute-done((bf16[2,6,4,4,1,1,128]{6,3,2,1,0,5,4:T(4,128)(2,1)S(1)}, bf16[2,6,4,4,1,1,128]{6,3,2,1,0,5,4:T(4,128)(2,1)S(1)}, u32[]{:S(2)}, u32[]{:S(2)}) %collective-permute-start.17) | collective-permute-done | bytes 49184 | tf_op jit(solution)/shard_map/ppermute | solution.py:21
  133.5 2.6 %collective-permute-done.19 = bf16[2,6,4,4,1,1,128]{6,3,2,1,0,5,4:T(4,128)(2,1)S(1)} collective-permute-done((bf16[2,6,4,4,1,1,128]{6,3,2,1,0,5,4:T(4,128)(2,1)S(1)}, bf16[2,6,4,4,1,1,128]{6,3,2,1,0,5,4:T(4,128)(2,1)S(1)}, u32[]{:S(2)}, u32[]{:S(2)}) %collective-permute-start.19) | collective-permute-done | bytes 49184 | tf_op jit(solution)/shard_map/ppermute | solution.py:21
  137.7 4.5 %collective-permute-start.20 = (bf16[2,6,4,4,1,1,128]{6,3,2,1,0,5,4:T(4,128)(2,1)S(1)}, bf16[2,6,4,4,1,1,128]{6,3,2,1,0,5,4:T(4,128)(2,1)S(1)}, u32[]{:S(2)}, u32[]{:S(2)}) collective-permute-start(bf16[2,6,4,4,1,1,128]{6,3,2,1,0,5,4:T(4,128)(2,1)S(1)} %get-tuple-element.147), channel_id=1, source_target_pairs={{0,16},{1,17},{2,18},{3,19},{4,20},{5,21},{6,22},{7,23},{8,24},{9,... | collective-permute-start | bytes 147464 | tf_op jit(solution)/shard_map/ppermute | solution.py:20
  143.5 4.4 %collective-permute-start.22 = (bf16[2,6,4,4,1,1,128]{6,3,2,1,0,5,4:T(4,128)(2,1)S(1)}, bf16[2,6,4,4,1,1,128]{6,3,2,1,0,5,4:T(4,128)(2,1)S(1)}, u32[]{:S(2)}, u32[]{:S(2)}) collective-permute-start(bf16[2,6,4,4,1,1,128]{6,3,2,1,0,5,4:T(4,128)(2,1)S(1)} %get-tuple-element.145), channel_id=1, source_target_pairs={{0,4},{4,8},{8,12},{1,5},{5,9},{9,13},{2,6},{6,10},{10,14},{3,7},{... | collective-permute-start | bytes 147464 | tf_op jit(solution)/shard_map/ppermute | solution.py:20
  153.6 4.8 %scatter_custom_fusion.3 = f32[6144]{0:T(1024)S(1)} fusion(s32[768]{0:T(1024)} %copy-done.16, f32[768]{0:T(1024)S(1)} %fusion.4, f32[]{:T(128)} %constant.129.clone.1), kind=kCustom, calls=%fused_computation.294 | custom fusion | flops 768 | bytes 25088 | tf_op jit(solution)/shard_map/scatter-add | solution.py:181
  158.4 11.0 %all_gather.7 = f32[8,1,16,384]{3,2,1,0:T(8,128)S(1)} all-gather(f32[1,1,16,384]{3,2,1,0:T(8,128)S(1)} %all_gather_reshape.7), channel_id=1, replica_groups=mesh['fx'=2,'fy'=4,'st'=4] {'fx','fy'}, dimensions={0}, use_global_device_ids=true | all-gather | bytes 221184 | tf_op jit(solution)/shard_map/all_gather | solution.py:183
  169.4 8.0 %all_to_all.42 = f32[1,16,384]{2,0,1:T(1,128)S(1)} all-to-all(f32[1,16,384]{2,0,1:T(1,128)S(1)} %reduce_sum.385), channel_id=1, replica_groups=mesh['fx'=2,'fy'=4,'st'=4] {'st'}, dimensions={1} | all-to-all | bytes 49152 | tf_op jit(solution)/shard_map/all_to_all | solution.py:184
  (274 shorter events, 48.0 us)
Async XLA Ops:
  0.7 28.4 %collective-permute-start = (bf16[2,6,4,4,1,1,128]{6,3,2,1,0,5,4:T(4,128)(2,1)S(1)}, bf16[2,6,4,4,1,1,128]{6,3,2,1,0,5,4:T(4,128)(2,1)S(1)}, u32[]{:S(2)}, u32[]{:S(2)}) collective-permute-start(bf16[2,6,4,4,1,1,128]{6,3,2,1,0,5,4:T(4,128)(2,1)S(1)} %get-tuple-element.197), channel_id=1, source_target_pairs={{0,16},{1,17},{2,18},{3,19},{4,20},{5,21},{6,22},{7,23},{8,24},{9,... | collective-permute-start | bytes 147464 | tf_op jit(solution)/shard_map/ppermute | solution.py:20
  5.8 23.3 %collective-permute-start.1 = (bf16[2,6,4,4,1,1,128]{6,3,2,1,0,5,4:T(4,128)(2,1)S(1)}, bf16[2,6,4,4,1,1,128]{6,3,2,1,0,5,4:T(4,128)(2,1)S(1)}, u32[]{:S(2)}, u32[]{:S(2)}) collective-permute-start(bf16[2,6,4,4,1,1,128]{6,3,2,1,0,5,4:T(4,128)(2,1)S(1)} %get-tuple-element.198), channel_id=1, source_target_pairs={{16,0},{17,1},{18,2},{19,3},{20,4},{21,5},{22,6},{23,7},{24,8},{25... | collective-permute-start | bytes 147464 | tf_op jit(solution)/shard_map/ppermute | solution.py:21
  7.1 22.0 %collective-permute-start.2 = (bf16[2,6,4,4,1,1,128]{6,3,2,1,0,5,4:T(4,128)(2,1)S(1)}, bf16[2,6,4,4,1,1,128]{6,3,2,1,0,5,4:T(4,128)(2,1)S(1)}, u32[]{:S(2)}, u32[]{:S(2)}) collective-permute-start(bf16[2,6,4,4,1,1,128]{6,3,2,1,0,5,4:T(4,128)(2,1)S(1)} %get-tuple-element.195), channel_id=1, source_target_pairs={{0,4},{4,8},{8,12},{1,5},{5,9},{9,13},{2,6},{6,10},{10,14},{3,7},{... | collective-permute-start | bytes 147464 | tf_op jit(solution)/shard_map/ppermute | solution.py:20
  8.6 20.5 %collective-permute-start.3 = (bf16[2,6,4,4,1,1,128]{6,3,2,1,0,5,4:T(4,128)(2,1)S(1)}, bf16[2,6,4,4,1,1,128]{6,3,2,1,0,5,4:T(4,128)(2,1)S(1)}, u32[]{:S(2)}, u32[]{:S(2)}) collective-permute-start(bf16[2,6,4,4,1,1,128]{6,3,2,1,0,5,4:T(4,128)(2,1)S(1)} %get-tuple-element.196), channel_id=1, source_target_pairs={{4,0},{8,4},{12,8},{5,1},{9,5},{13,9},{6,2},{10,6},{14,10},{7,3},{... | collective-permute-start | bytes 147464 | tf_op jit(solution)/shard_map/ppermute | solution.py:21
  11.7 10.5 %all-to-all-start = ((bf16[4,4,384]{2,1,0:T(4,128)(2,1)}), bf16[4,4,384]{2,1,0:T(4,128)(2,1)S(1)}, u32[]{:S(2)}, u32[]{:S(2)}) async-start(bf16[4,4,384]{2,1,0:T(4,128)(2,1)} %copy.260), calls=%async_computation | async-start | bytes 24576 | tf_op jit(solution)/shard_map/all_to_all | solution.py:155
  19.7 54.3 %copy-start.21 = (s32[1024]{0:T(1024)}, s32[1024]{0:T(1024)S(1)}, u32[]{:S(2)}) copy-start(s32[1024]{0:T(1024)S(1)} %pad_clamp_fusion) | copy-start | bytes 12292
  31.5 10.2 %collective-permute-start.4 = (bf16[2,6,4,4,1,1,128]{6,3,2,1,0,5,4:T(4,128)(2,1)S(1)}, bf16[2,6,4,4,1,1,128]{6,3,2,1,0,5,4:T(4,128)(2,1)S(1)}, u32[]{:S(2)}, u32[]{:S(2)}) collective-permute-start(bf16[2,6,4,4,1,1,128]{6,3,2,1,0,5,4:T(4,128)(2,1)S(1)} %get-tuple-element.187), channel_id=1, source_target_pairs={{0,16},{1,17},{2,18},{3,19},{4,20},{5,21},{6,22},{7,23},{8,24},{9,... | collective-permute-start | bytes 147464 | tf_op jit(solution)/shard_map/ppermute | solution.py:20
  35.9 6.3 %collective-permute-start.5 = (bf16[2,6,4,4,1,1,128]{6,3,2,1,0,5,4:T(4,128)(2,1)S(1)}, bf16[2,6,4,4,1,1,128]{6,3,2,1,0,5,4:T(4,128)(2,1)S(1)}, u32[]{:S(2)}, u32[]{:S(2)}) collective-permute-start(bf16[2,6,4,4,1,1,128]{6,3,2,1,0,5,4:T(4,128)(2,1)S(1)} %get-tuple-element.188), channel_id=1, source_target_pairs={{16,0},{17,1},{18,2},{19,3},{20,4},{21,5},{22,6},{23,7},{24,8},{25... | collective-permute-start | bytes 147464 | tf_op jit(solution)/shard_map/ppermute | solution.py:21
  37.2 5.0 %collective-permute-start.6 = (bf16[2,6,4,4,1,1,128]{6,3,2,1,0,5,4:T(4,128)(2,1)S(1)}, bf16[2,6,4,4,1,1,128]{6,3,2,1,0,5,4:T(4,128)(2,1)S(1)}, u32[]{:S(2)}, u32[]{:S(2)}) collective-permute-start(bf16[2,6,4,4,1,1,128]{6,3,2,1,0,5,4:T(4,128)(2,1)S(1)} %get-tuple-element.185), channel_id=1, source_target_pairs={{0,4},{4,8},{8,12},{1,5},{5,9},{9,13},{2,6},{6,10},{10,14},{3,7},{... | collective-permute-start | bytes 147464 | tf_op jit(solution)/shard_map/ppermute | solution.py:20
  40.3 6.1 %collective-permute-start.7 = (bf16[2,6,4,4,1,1,128]{6,3,2,1,0,5,4:T(4,128)(2,1)S(1)}, bf16[2,6,4,4,1,1,128]{6,3,2,1,0,5,4:T(4,128)(2,1)S(1)}, u32[]{:S(2)}, u32[]{:S(2)}) collective-permute-start(bf16[2,6,4,4,1,1,128]{6,3,2,1,0,5,4:T(4,128)(2,1)S(1)} %get-tuple-element.186), channel_id=1, source_target_pairs={{4,0},{8,4},{12,8},{5,1},{9,5},{13,9},{6,2},{10,6},{14,10},{7,3},{... | collective-permute-start | bytes 147464 | tf_op jit(solution)/shard_map/ppermute | solution.py:21
  48.7 12.0 %collective-permute-start.10 = (bf16[2,6,4,4,1,1,128]{6,3,2,1,0,5,4:T(4,128)(2,1)S(1)}, bf16[2,6,4,4,1,1,128]{6,3,2,1,0,5,4:T(4,128)(2,1)S(1)}, u32[]{:S(2)}, u32[]{:S(2)}) collective-permute-start(bf16[2,6,4,4,1,1,128]{6,3,2,1,0,5,4:T(4,128)(2,1)S(1)} %get-tuple-element.175), channel_id=1, source_target_pairs={{0,4},{4,8},{8,12},{1,5},{5,9},{9,13},{2,6},{6,10},{10,14},{3,7},{... | collective-permute-start | bytes 147464 | tf_op jit(solution)/shard_map/ppermute | solution.py:20
  53.4 7.3 %collective-permute-start.11 = (bf16[2,6,4,4,1,1,128]{6,3,2,1,0,5,4:T(4,128)(2,1)S(1)}, bf16[2,6,4,4,1,1,128]{6,3,2,1,0,5,4:T(4,128)(2,1)S(1)}, u32[]{:S(2)}, u32[]{:S(2)}) collective-permute-start(bf16[2,6,4,4,1,1,128]{6,3,2,1,0,5,4:T(4,128)(2,1)S(1)} %get-tuple-element.176), channel_id=1, source_target_pairs={{4,0},{8,4},{12,8},{5,1},{9,5},{13,9},{6,2},{10,6},{14,10},{7,3},{... | collective-permute-start | bytes 147464 | tf_op jit(solution)/shard_map/ppermute | solution.py:21
  54.7 6.5 %collective-permute-start.8 = (bf16[2,6,4,4,1,1,128]{6,3,2,1,0,5,4:T(4,128)(2,1)S(1)}, bf16[2,6,4,4,1,1,128]{6,3,2,1,0,5,4:T(4,128)(2,1)S(1)}, u32[]{:S(2)}, u32[]{:S(2)}) collective-permute-start(bf16[2,6,4,4,1,1,128]{6,3,2,1,0,5,4:T(4,128)(2,1)S(1)} %get-tuple-element.177), channel_id=1, source_target_pairs={{0,16},{1,17},{2,18},{3,19},{4,20},{5,21},{6,22},{7,23},{8,24},{9,... | collective-permute-start | bytes 147464 | tf_op jit(solution)/shard_map/ppermute | solution.py:20
  59.3 6.4 %collective-permute-start.9 = (bf16[2,6,4,4,1,1,128]{6,3,2,1,0,5,4:T(4,128)(2,1)S(1)}, bf16[2,6,4,4,1,1,128]{6,3,2,1,0,5,4:T(4,128)(2,1)S(1)}, u32[]{:S(2)}, u32[]{:S(2)}) collective-permute-start(bf16[2,6,4,4,1,1,128]{6,3,2,1,0,5,4:T(4,128)(2,1)S(1)} %get-tuple-element.178), channel_id=1, source_target_pairs={{16,0},{17,1},{18,2},{19,3},{20,4},{21,5},{22,6},{23,7},{24,8},{25... | collective-permute-start | bytes 147464 | tf_op jit(solution)/shard_map/ppermute | solution.py:21
  70.3 24.0 %copy-start.6 = (bf16[1,6,64,1,1,128]{5,2,4,3,1,0:T(8,128)(2,1)S(1)}, bf16[1,6,64,1,1,128]{5,2,4,3,1,0:T(8,128)(2,1)}, u32[]{:S(2)}) copy-start(bf16[1,6,64,1,1,128]{5,2,4,3,1,0:T(8,128)(2,1)} %param.27) | copy-start | bytes 294916
  70.3 24.0 %copy-start.15 = (f32[6,1,1,128]{3,0,1,2:T(8,128)S(1)}, f32[6,1,1,128]{3,0,1,2:T(8,128)}, u32[]{:S(2)}) copy-start(f32[6,1,1,128]{3,0,1,2:T(8,128)} %copy.475) | copy-start | bytes 9220
  71.8 36.9 %collective-permute-start.12 = (bf16[2,6,4,4,1,1,128]{6,3,2,1,0,5,4:T(4,128)(2,1)}, bf16[2,6,4,4,1,1,128]{6,3,2,1,0,5,4:T(4,128)(2,1)}, u32[]{:S(2)}, u32[]{:S(2)}) collective-permute-start(bf16[2,6,4,4,1,1,128]{6,3,2,1,0,5,4:T(4,128)(2,1)} %get-tuple-element.167), channel_id=1, source_target_pairs={{0,16},{1,17},{2,18},{3,19},{4,20},{5,21},{6,22},{7,23},{8,24},{9,... | collective-permute-start | bytes 147464 | tf_op jit(solution)/shard_map/ppermute | solution.py:20
  90.4 9.9 %all-to-all-start.1 = ((f32[1,16,384]{2,0,1:T(1,128)}), f32[1,16,384]{2,0,1:T(1,128)}, u32[]{:S(2)}, u32[]{:S(2)}) async-start(f32[1,16,384]{2,0,1:T(1,128)} %reduce_sum.365), calls=%async_computation.1 | async-start | bytes 49152 | tf_op jit(solution)/shard_map/all_to_all | solution.py:184
  95.4 13.4 %collective-permute-start.13 = (bf16[2,6,4,4,1,1,128]{6,3,2,1,0,5,4:T(4,128)(2,1)}, bf16[2,6,4,4,1,1,128]{6,3,2,1,0,5,4:T(4,128)(2,1)S(1)}, u32[]{:S(2)}, u32[]{:S(2)}) collective-permute-start(bf16[2,6,4,4,1,1,128]{6,3,2,1,0,5,4:T(4,128)(2,1)} %get-tuple-element.168), channel_id=1, source_target_pairs={{16,0},{17,1},{18,2},{19,3},{20,4},{21,5},{22,6},{23,7},{24,8},{25... | collective-permute-start | bytes 147464 | tf_op jit(solution)/shard_map/ppermute | solution.py:21
  96.7 12.1 %collective-permute-start.14 = (bf16[2,6,4,4,1,1,128]{6,3,2,1,0,5,4:T(4,128)(2,1)}, bf16[2,6,4,4,1,1,128]{6,3,2,1,0,5,4:T(4,128)(2,1)S(1)}, u32[]{:S(2)}, u32[]{:S(2)}) collective-permute-start(bf16[2,6,4,4,1,1,128]{6,3,2,1,0,5,4:T(4,128)(2,1)} %get-tuple-element.165), channel_id=1, source_target_pairs={{0,4},{4,8},{8,12},{1,5},{5,9},{9,13},{2,6},{6,10},{10,14},{3,7},{... | collective-permute-start | bytes 147464 | tf_op jit(solution)/shard_map/ppermute | solution.py:20
  98.9 9.8 %collective-permute-start.15 = (bf16[2,6,4,4,1,1,128]{6,3,2,1,0,5,4:T(4,128)(2,1)}, bf16[2,6,4,4,1,1,128]{6,3,2,1,0,5,4:T(4,128)(2,1)S(1)}, u32[]{:S(2)}, u32[]{:S(2)}) collective-permute-start(bf16[2,6,4,4,1,1,128]{6,3,2,1,0,5,4:T(4,128)(2,1)} %get-tuple-element.166), channel_id=1, source_target_pairs={{4,0},{8,4},{12,8},{5,1},{9,5},{13,9},{6,2},{10,6},{14,10},{7,3},{... | collective-permute-start | bytes 147464 | tf_op jit(solution)/shard_map/ppermute | solution.py:21
  104.0 10.3 %all-to-all-start.2 = ((bf16[4,4,384]{2,1,0:T(4,128)(2,1)}), bf16[4,4,384]{2,1,0:T(4,128)(2,1)S(1)}, u32[]{:S(2)}, u32[]{:S(2)}) async-start(bf16[4,4,384]{2,1,0:T(4,128)(2,1)} %copy.301), calls=%async_computation.2 | async-start | bytes 24576 | tf_op jit(solution)/shard_map/all_to_all | solution.py:155
  123.2 8.3 %collective-permute-start.16 = (bf16[2,6,4,4,1,1,128]{6,3,2,1,0,5,4:T(4,128)(2,1)S(1)}, bf16[2,6,4,4,1,1,128]{6,3,2,1,0,5,4:T(4,128)(2,1)S(1)}, u32[]{:S(2)}, u32[]{:S(2)}) collective-permute-start(bf16[2,6,4,4,1,1,128]{6,3,2,1,0,5,4:T(4,128)(2,1)S(1)} %get-tuple-element.157), channel_id=1, source_target_pairs={{0,16},{1,17},{2,18},{3,19},{4,20},{5,21},{6,22},{7,23},{8,24},{9,... | collective-permute-start | bytes 147464 | tf_op jit(solution)/shard_map/ppermute | solution.py:20
  127.5 6.0 %collective-permute-start.17 = (bf16[2,6,4,4,1,1,128]{6,3,2,1,0,5,4:T(4,128)(2,1)S(1)}, bf16[2,6,4,4,1,1,128]{6,3,2,1,0,5,4:T(4,128)(2,1)S(1)}, u32[]{:S(2)}, u32[]{:S(2)}) collective-permute-start(bf16[2,6,4,4,1,1,128]{6,3,2,1,0,5,4:T(4,128)(2,1)S(1)} %get-tuple-element.158), channel_id=1, source_target_pairs={{16,0},{17,1},{18,2},{19,3},{20,4},{21,5},{22,6},{23,7},{24,8},{25... | collective-permute-start | bytes 147464 | tf_op jit(solution)/shard_map/ppermute | solution.py:21
  128.8 4.7 %collective-permute-start.18 = (bf16[2,6,4,4,1,1,128]{6,3,2,1,0,5,4:T(4,128)(2,1)S(1)}, bf16[2,6,4,4,1,1,128]{6,3,2,1,0,5,4:T(4,128)(2,1)S(1)}, u32[]{:S(2)}, u32[]{:S(2)}) collective-permute-start(bf16[2,6,4,4,1,1,128]{6,3,2,1,0,5,4:T(4,128)(2,1)S(1)} %get-tuple-element.155), channel_id=1, source_target_pairs={{0,4},{4,8},{8,12},{1,5},{5,9},{9,13},{2,6},{6,10},{10,14},{3,7},{... | collective-permute-start | bytes 147464 | tf_op jit(solution)/shard_map/ppermute | solution.py:20
  130.1 5.9 %collective-permute-start.19 = (bf16[2,6,4,4,1,1,128]{6,3,2,1,0,5,4:T(4,128)(2,1)S(1)}, bf16[2,6,4,4,1,1,128]{6,3,2,1,0,5,4:T(4,128)(2,1)S(1)}, u32[]{:S(2)}, u32[]{:S(2)}) collective-permute-start(bf16[2,6,4,4,1,1,128]{6,3,2,1,0,5,4:T(4,128)(2,1)S(1)} %get-tuple-element.156), channel_id=1, source_target_pairs={{4,0},{8,4},{12,8},{5,1},{9,5},{13,9},{6,2},{10,6},{14,10},{7,3},{... | collective-permute-start | bytes 147464 | tf_op jit(solution)/shard_map/ppermute | solution.py:21
  137.7 12.4 %collective-permute-start.20 = (bf16[2,6,4,4,1,1,128]{6,3,2,1,0,5,4:T(4,128)(2,1)S(1)}, bf16[2,6,4,4,1,1,128]{6,3,2,1,0,5,4:T(4,128)(2,1)S(1)}, u32[]{:S(2)}, u32[]{:S(2)}) collective-permute-start(bf16[2,6,4,4,1,1,128]{6,3,2,1,0,5,4:T(4,128)(2,1)S(1)} %get-tuple-element.147), channel_id=1, source_target_pairs={{0,16},{1,17},{2,18},{3,19},{4,20},{5,21},{6,22},{7,23},{8,24},{9,... | collective-permute-start | bytes 147464 | tf_op jit(solution)/shard_map/ppermute | solution.py:20
  142.2 7.8 %collective-permute-start.21 = (bf16[2,6,4,4,1,1,128]{6,3,2,1,0,5,4:T(4,128)(2,1)S(1)}, bf16[2,6,4,4,1,1,128]{6,3,2,1,0,5,4:T(4,128)(2,1)S(1)}, u32[]{:S(2)}, u32[]{:S(2)}) collective-permute-start(bf16[2,6,4,4,1,1,128]{6,3,2,1,0,5,4:T(4,128)(2,1)S(1)} %get-tuple-element.148), channel_id=1, source_target_pairs={{16,0},{17,1},{18,2},{19,3},{20,4},{21,5},{22,6},{23,7},{24,8},{25... | collective-permute-start | bytes 147464 | tf_op jit(solution)/shard_map/ppermute | solution.py:21
  143.5 6.5 %collective-permute-start.22 = (bf16[2,6,4,4,1,1,128]{6,3,2,1,0,5,4:T(4,128)(2,1)S(1)}, bf16[2,6,4,4,1,1,128]{6,3,2,1,0,5,4:T(4,128)(2,1)S(1)}, u32[]{:S(2)}, u32[]{:S(2)}) collective-permute-start(bf16[2,6,4,4,1,1,128]{6,3,2,1,0,5,4:T(4,128)(2,1)S(1)} %get-tuple-element.145), channel_id=1, source_target_pairs={{0,4},{4,8},{8,12},{1,5},{5,9},{9,13},{2,6},{6,10},{10,14},{3,7},{... | collective-permute-start | bytes 147464 | tf_op jit(solution)/shard_map/ppermute | solution.py:20
  147.9 3.1 %collective-permute-start.23 = (bf16[2,6,4,4,1,1,128]{6,3,2,1,0,5,4:T(4,128)(2,1)S(1)}, bf16[2,6,4,4,1,1,128]{6,3,2,1,0,5,4:T(4,128)(2,1)S(1)}, u32[]{:S(2)}, u32[]{:S(2)}) collective-permute-start(bf16[2,6,4,4,1,1,128]{6,3,2,1,0,5,4:T(4,128)(2,1)S(1)} %get-tuple-element.146), channel_id=1, source_target_pairs={{4,0},{8,4},{12,8},{5,1},{9,5},{13,9},{6,2},{10,6},{14,10},{7,3},{... | collective-permute-start | bytes 147464 | tf_op jit(solution)/shard_map/ppermute | solution.py:21
  151.6 25.8 %copy-start.11 = (f32[4,4,384]{2,1,0:T(4,128)S(1)}, f32[4,4,384]{2,1,0:T(4,128)}, u32[]{:S(2)}) copy-start(f32[4,4,384]{2,1,0:T(4,128)} %param.35) | copy-start | bytes 73732
  153.5 24.5 %copy-start.9 = (f32[4,4,384]{2,1,0:T(4,128)S(1)}, f32[4,4,384]{2,1,0:T(4,128)}, u32[]{:S(2)}) copy-start(f32[4,4,384]{2,1,0:T(4,128)} %param.34) | copy-start | bytes 73732
  (21 other events, 133.4 us)
